TPU v7x, 32 devices: a whole 2x2x4 slice. The times are simulated.
32 devices in a mesh: row: 4 (over x, core), col: 2 (over y), depth: 4 (over z).
Axes of the slice: x: 2, y: 2, z: 4, core: 2. Of those that a mesh axis runs over, the one named last changes fastest.
Arguments:
- tokens: bfloat16 [64, 6144], P(('col', 'depth'), 'row'), may hold values from -6 to 6
- first_weight: bfloat16 [6144, 24576], P('row', ('col', 'depth')), may hold values from -0.078125 to 0.078125
- first_tangent: bfloat16 [6144, 24576], P('row', ('col', 'depth')), may hold values from -0.078125 to 0.078125
- second_weight: bfloat16 [24576, 6144], P(('col', 'depth'), 'row'), may hold values from -0.0390625 to 0.0390625
- second_tangent: bfloat16 [24576, 6144], P(('col', 'depth'), 'row'), may hold values from -0.0390625 to 0.0390625
Outputs:
- grad_first: float32 [6144, 24576], P('row', ('col', 'depth'))
- grad_second: float32 [24576, 6144], P(('col', 'depth'), 'row')
All inputs are finite; a program needn't handle non-finite values.
Results may differ from a plain program's by a relative error of at most 0.0047.
Values may be sent and summed in bfloat16 or wider, within the bound.
A program may use at most 192 MiB of HBM per device.

v0:
```python
import math
import jax
import jax.numpy as jnp
from jax import lax
from jax.sharding import PartitionSpec as P


def gelu_parts(hidden, hidden_tan):
    inner = 0.7978845608 * (hidden + 0.044715 * hidden * hidden * hidden)
    tval = jnp.tanh(inner)
    active = (0.5 * hidden * (1.0 + tval)).astype(jnp.bfloat16)
    slopes = 0.5 * (1.0 + tval) + 0.5 * hidden * (1.0 - tval * tval) * 0.7978845608 * (
        1.0 + 3.0 * 0.044715 * hidden * hidden
    )
    active_tan = (slopes * hidden_tan).astype(jnp.bfloat16)
    return (active, active_tan, slopes)


def on_device(tokens, first_weight, first_tangent, second_weight, second_tangent):
    gathered = lax.all_gather(tokens, ("col", "depth"), axis=0, tiled=True)
    hidden = jnp.dot(gathered, first_weight, preferred_element_type=jnp.float32)
    hidden_tan = jnp.dot(gathered, first_tangent, preferred_element_type=jnp.float32)
    hidden, hidden_tan = lax.psum((hidden, hidden_tan), "row")
    active, active_tan, slopes = gelu_parts(hidden, hidden_tan)
    partial_value = jnp.dot(
        active_tan, second_weight, preferred_element_type=jnp.float32
    ) + jnp.dot(active, second_tangent, preferred_element_type=jnp.float32)
    out_tan = lax.psum(partial_value, ("col", "depth")).astype(jnp.bfloat16)
    backward = lax.dot_general(
        out_tan, second_weight, (((1,), (1,)), ((), ())), preferred_element_type=jnp.float32
    )
    backward = lax.psum(backward, "row")
    back_hidden = (backward * slopes).astype(jnp.bfloat16)
    factor = 1.0 / math.sqrt(gathered.shape[0])
    grad_second = (
        lax.dot_general(
            active, out_tan, (((0,), (0,)), ((), ())), preferred_element_type=jnp.float32
        )
        * factor
    )
    grad_first = (
        lax.dot_general(
            gathered, back_hidden, (((0,), (0,)), ((), ())), preferred_element_type=jnp.float32
        )
        * factor
    )
    return (grad_first, grad_second)


def solution(mesh):
    return jax.shard_map(
        on_device,
        mesh=mesh,
        in_specs=(
            P(("col", "depth"), "row"),
            P("row", ("col", "depth")),
            P("row", ("col", "depth")),
            P(("col", "depth"), "row"),
            P(("col", "depth"), "row"),
        ),
        out_specs=(P("row", ("col", "depth")), P(("col", "depth"), "row")),
        check_vma=False,
    )
```

profile of v0, /device:TPU:0, one launch (start us, length us, event | category | flops | bytes accessed | tf_op | source)
XLA Modules:
  0.0 220.9 jit_solution(1123703977794834401)
XLA Ops:
  7.2 0.0 slice-start.3
  7.2 0.0 all-reduce.7.cloned.1.call-start
  7.2 33.1 %all_gather.3 = bf16[64,1536]{1,0:T(8,128)(2,1)S(1)} all-gather(bf16[8,1536]{1,0:T(8,128)(2,1)} %param.5), channel_id=1, replica_groups=mesh['row'=4,'col'=2,'depth'=4] {'col','depth'}, dimensions={0}, use_global_device_ids=true | all-gather | bytes 221184 | tf_op jit(solution)/shard_map/all_gather | solution.py:20
  40.3 0.0 slice-start.4
  40.3 0.0 slice-start.5
  40.3 6.5 %fusion.12 = f32[64,3072]{1,0:T(8,128)} fusion(bf16[64,1536]{1,0:T(8,128)(2,1)S(1)} %all_gather.3, bf16[1536,3072]{1,0:T(8,128)(2,1)} %param.7), kind=kOutput, calls=%fused_computation.18 | convolution fusion | flops 603979776 | bytes 10420224 | tf_op jit(solution)/shard_map/dot_general | solution.py:22
  46.8 0.0 slice-done.3
  46.8 0.0 slice-done.4
  46.8 0.0 slice-done.5
  46.8 2.6 %fusion.11 = f32[64,3072]{1,0:T(8,128)} fusion(bf16[64,1536]{1,0:T(8,128)(2,1)S(1)} %all_gather.3, bf16[1536,3072]{1,0:T(8,128)(2,1)S(1)} %bitcast.15), kind=kOutput, calls=%fused_computation.17 | convolution fusion | flops 603979776 | bytes 10420224 | tf_op jit(solution)/shard_map/dot_general | solution.py:21
  49.4 0.0 slice-start
  49.4 0.0 all-reduce.7.cloned.1.call-update
  49.5 0.0 all-reduce.5.cloned.1.call-start
  49.5 44.0 %all-reduce.7.cloned.1.call-done = (f32[64,3072]{1,0:T(8,128)}, f32[64,3072]{1,0:T(8,128)}) async-done(((f32[64,3072]{1,0:T(8,128)}, f32[64,3072]{1,0:T(8,128)}), (f32[64,3072]{1,0:T(8,128)}, f32[64,3072]{1,0:T(8,128)})) %all-reduce.7.cloned.1.call-update) | async-done | bytes 1572880 | tf_op jit(solution)/shard_map/psum | solution.py:23
  93.5 0.0 slice-start.1
  93.5 0.0 slice-start.2
  93.5 0.0 copy-start
  93.5 6.3 %fusion.5 = f32[64,1536]{1,0:T(8,128)S(1)} fusion(bf16[3072,1536]{1,0:T(8,128)(2,1)} %param.8, f32[64,3072]{1,0:T(8,128)} %get-tuple-element.4, f32[64,3072]{1,0:T(8,128)} %get-tuple-element.5), kind=kOutput, calls=%fused_computation.13 | convolution fusion | flops 607715328 | bytes 11403264 | tf_op jit(solution)/shard_map/dot_general | solution.py:25
  99.8 0.0 slice-done
  99.8 0.0 slice-done.1
  99.8 0.3 slice-done.2
  100.1 0.1 copy-done
  100.2 1.8 convolution_add_fusion
  102.0 44.5 %all-reduce.8 = bf16[64,1536]{1,0:T(8,128)(2,1)S(1)} all-reduce(f32[64,1536]{1,0:T(8,128)S(1)} %convolution_add_fusion), channel_id=1, replica_groups=mesh['row'=4,'col'=2,'depth'=4] {'col','depth'}, use_global_device_ids=true, to_apply=%region_2.0 | all-reduce | flops 98304 | bytes 589824 | tf_op jit(solution)/shard_map/psum | solution.py:28
  146.5 7.5 %fusion.13 = f32[64,3072]{1,0:T(8,128)} fusion(bf16[64,1536]{1,0:T(8,128)(2,1)S(1)} %all-reduce.8, bf16[3072,1536]{1,0:T(8,128)(2,1)} %param.8), kind=kOutput, calls=%fused_computation.19 | convolution fusion | flops 603979776 | bytes 10420224 | tf_op jit(solution)/shard_map/dot_general | solution.py:29
  154.0 0.0 all-reduce.5.cloned.1.call-update
  154.0 8.3 %convolution_multiply_fusion = f32[3072,1536]{1,0:T(8,128)} fusion(bf16[64,1536]{1,0:T(8,128)(2,1)S(1)} %all-reduce.8, f32[64,3072]{1,0:T(8,128)S(1)} %copy-done), kind=kOutput, calls=%fused_computation.1 | convolution fusion | flops 610467840 | bytes 19857408 | tf_op jit(solution)/shard_map/dot_general | solution.py:36
  162.3 23.6 %all-reduce.5.cloned.1.call-done = f32[64,3072]{1,0:T(8,128)} async-done(((f32[64,3072]{1,0:T(8,128)}), f32[64,3072]{1,0:T(8,128)}) %all-reduce.5.cloned.1.call-update) | async-done | bytes 786448 | tf_op jit(solution)/shard_map/psum | solution.py:32
  185.9 9.6 %multiply_bitcast_fusion = f32[1536,3072]{0,1:T(8,128)} fusion(bf16[64,1536]{1,0:T(8,128)(2,1)S(1)} %all_gather.3, f32[64,3072]{1,0:T(8,128)} %all-reduce.5.cloned.1.call-done, f32[64,3072]{1,0:T(8,128)S(1)} %copy-done), kind=kOutput, calls=%fused_computation | convolution fusion | flops 612433920 | bytes 20643840 | tf_op jit(solution)/shard_map/dot_general | solution.py:42
  195.4 18.6 %copy.7 = f32[1536,3072]{1,0:T(8,128)} copy(f32[1536,3072]{0,1:T(8,128)} %multiply_bitcast_fusion) | data formatting | bytes 37748736
  (2 shorter events, 0.0 us)
Async XLA Ops:
  7.2 39.6 %slice-start.3 = ((s8[9437184]{0:T(1024)(128)(4,1)}), s8[1048576]{0:T(1024)(128)(4,1)S(1)}, s32[]{:S(2)}) async-start(s8[9437184]{0:T(1024)(128)(4,1)} %bitcast.14), calls=%async_computation.5 | async-start | bytes 2097152
  7.2 86.3 %all-reduce.7.cloned.1.call-start = ((), (), s32[]{:S(2)}) async-start(), calls=%async_computation.1 | async-start | bytes 3145728 | tf_op jit(solution)/shard_map/psum | solution.py:23
  40.3 6.5 %slice-start.4 = ((s8[9437184]{0:T(1024)(128)(4,1)}), s8[4194304]{0:T(1024)(128)(4,1)S(1)}, s32[]{:S(2)}) async-start(s8[9437184]{0:T(1024)(128)(4,1)} %bitcast.14), calls=%async_computation.6 | async-start | bytes 8388608
  40.3 6.5 %slice-start.5 = ((s8[9437184]{0:T(1024)(128)(4,1)}), s8[4194304]{0:T(1024)(128)(4,1)S(1)}, s32[]{:S(2)}) async-start(s8[9437184]{0:T(1024)(128)(4,1)} %bitcast.14), calls=%async_computation.7 | async-start | bytes 8388608
  49.4 50.3 %slice-start = ((s8[9437184]{0:T(1024)(128)(4,1)}), s8[1048576]{0:T(1024)(128)(4,1)S(1)}, s32[]{:S(2)}) async-start(s8[9437184]{0:T(1024)(128)(4,1)} %bitcast.12), calls=%async_computation.2 | async-start | bytes 2097152
  49.5 136.4 %all-reduce.5.cloned.1.call-start = ((), (), s32[]{:S(2)}) async-start(), calls=%async_computation | async-start | bytes 1572864 | tf_op jit(solution)/shard_map/psum | solution.py:32
  93.5 6.3 %slice-start.1 = ((s8[9437184]{0:T(1024)(128)(4,1)}), s8[4194304]{0:T(1024)(128)(4,1)S(1)}, s32[]{:S(2)}) async-start(s8[9437184]{0:T(1024)(128)(4,1)} %bitcast.12), calls=%async_computation.3 | async-start | bytes 8388608
  93.5 6.6 %slice-start.2 = ((s8[9437184]{0:T(1024)(128)(4,1)}), s8[4194304]{0:T(1024)(128)(4,1)S(1)}, s32[]{:S(2)}) async-start(s8[9437184]{0:T(1024)(128)(4,1)} %bitcast.12), calls=%async_computation.4 | async-start | bytes 8388608
  93.5 6.7 %copy-start = (f32[64,3072]{1,0:T(8,128)S(1)}, f32[64,3072]{1,0:T(8,128)}, u32[]{:S(2)}) copy-start(f32[64,3072]{1,0:T(8,128)} %get-tuple-element.5) | copy-start | bytes 2359300
Sparse Core Ops, SparseCore 0:
  49.6 43.8 all-reduce.6
  154.1 31.7 all-reduce.4
where the time goes:
time: 221 us
  blocking collectives  77.6 us (35%)
  waiting for transfers between devices  67.6 us (31%)
  matrix products  42.5 us (19%)
  local copies, waits for them, and re-layouts  19.1 us (9%)
  between operations  14.1 us (6%)
    psum x1, blocking collectives, on_device(): out_tan = lax.psum(partial_value, ('col', 'depth')).astype(jnp.bfloat16)  44.5 us
    psum x1, waiting for transfers between devices, on_device(): hidden, hidden_tan = lax.psum((hidden, hidden_tan), 'row')  44 us
    all_gather x1, blocking collectives, on_device(): gathered = lax.all_gather(tokens, ('col', 'depth'), axis=0, tiled=True)  33.1 us
    psum x1, waiting for transfers between devices, on_device(): backward = lax.psum(backward, 'row')  23.6 us
    unnamed x15, local copies, waits for them, and re-layouts  19.1 us
    dot_general x1, matrix products, on_device(): lax.dot_general(gathered, back_hidden, (((0,), (0,)), ((), ())), preferre...  9.56 us
    dot_general x1, matrix products, on_device(): lax.dot_general(active, out_tan, (((0,), (0,)), ((), ())), preferred_elem...  8.3 us
    dot_general x1, matrix products, on_device(): lax.dot_general(out_tan, second_weight, (((1,), (1,)), ((), ())), preferr...  7.5 us
  transfers between devices with their start and end apart: 2, of which 2 were waited for; matrix products, arithmetic and copies ran while one was open for 4% of the time, Pallas kernels for 0%

commit v1 on v0

--- a/solution.py
+++ b/solution.py
@@ -29,7 +29,9 @@
     backward = lax.dot_general(
         out_tan, second_weight, (((1,), (1,)), ((), ())), preferred_element_type=jnp.float32
     )
-    backward = lax.psum(backward, "row")
+    backward = backward
+    for hop in (1, 2):
+        backward = backward + lax.ppermute(backward, "row", [(dev, dev ^ hop) for dev in range(4)])
     back_hidden = (backward * slopes).astype(jnp.bfloat16)
     factor = 1.0 / math.sqrt(gathered.shape[0])
     grad_second = (

time: 221 us -> 209 us (0.946)
  waiting for transfers between devices: 67.6 us -> 57 us
  matrix products: 42.5 us -> 39.9 us
    psum x1 -> x0, waiting for transfers between devices: 23.6 us -> none  [on_device(): backward = lax.psum(backward, 'row')]
    ppermute x0 -> x2, waiting for transfers between devices: none -> 12.9 us  [on_device(): lax.ppermute(backward, 'row', [(dev, dev ^ hop) for dev in range(4)])]
  transfers between devices with their start and end apart: 2 -> 3, of which waited for: 2 -> 3; matrix products, arithmetic and copies ran while one was open for 4% -> 4% of each run, Pallas kernels for 0% -> 0%
where the time goes in v1:
time: 209 us
  blocking collectives  77.6 us (37%)
  waiting for transfers between devices  57 us (27%)
  matrix products  39.9 us (19%)
  local copies, waits for them, and re-layouts  19.1 us (9%)
  between operations  14.1 us (7%)
    psum x1, blocking collectives, on_device(): out_tan = lax.psum(partial_value, ('col', 'depth')).astype(jnp.bfloat16)  44.5 us
    psum x1, waiting for transfers between devices, on_device(): hidden, hidden_tan = lax.psum((hidden, hidden_tan), 'row')  44 us
    all_gather x1, blocking collectives, on_device(): gathered = lax.all_gather(tokens, ('col', 'depth'), axis=0, tiled=True)  33.1 us
    unnamed x15, local copies, waits for them, and re-layouts  19.1 us
    ppermute x2, waiting for transfers between devices, on_device(): lax.ppermute(backward, 'row', [(dev, dev ^ hop) for dev in range(4)])  12.9 us
    dot_general x1, matrix products, on_device(): lax.dot_general(active, out_tan, (((0,), (0,)), ((), ())), preferred_elem...  8.28 us
    dot_general x1, matrix products, on_device(): lax.dot_general(gathered, back_hidden, (((0,), (0,)), ((), ())), preferre...  7.91 us
    dot_general x1, matrix products, on_device(): lax.dot_general(out_tan, second_weight, (((1,), (1,)), ((), ())), preferr...  6.61 us
  transfers between devices with their start and end apart: 3, of which 3 were waited for; matrix products, arithmetic and copies ran while one was open for 4% of the time, Pallas kernels for 0%

profile of v1, /device:TPU:0, one launch (start us, length us, event | category | flops | bytes accessed | tf_op | source)
XLA Modules:
  0.0 208.6 jit_solution(10201613922126537078)
XLA Ops:
  7.2 0.0 slice-start.3
  7.2 0.0 all-reduce.4.cloned.1.call-start
  7.2 33.1 %all_gather.3 = bf16[64,1536]{1,0:T(8,128)(2,1)S(1)} all-gather(bf16[8,1536]{1,0:T(8,128)(2,1)} %param.5), channel_id=1, replica_groups=mesh['row'=4,'col'=2,'depth'=4] {'col','depth'}, dimensions={0}, use_global_device_ids=true | all-gather | bytes 221184 | tf_op jit(solution)/shard_map/all_gather | solution.py:20
  40.3 0.0 slice-start.4
  40.3 0.0 slice-start.5
  40.3 6.5 %fusion.12 = f32[64,3072]{1,0:T(8,128)} fusion(bf16[64,1536]{1,0:T(8,128)(2,1)S(1)} %all_gather.3, bf16[1536,3072]{1,0:T(8,128)(2,1)} %param.7), kind=kOutput, calls=%fused_computation.18 | convolution fusion | flops 603979776 | bytes 10420224 | tf_op jit(solution)/shard_map/dot_general | solution.py:22
  46.8 0.0 slice-done.3
  46.8 0.0 slice-done.4
  46.8 0.0 slice-done.5
  46.8 2.6 %fusion.11 = f32[64,3072]{1,0:T(8,128)} fusion(bf16[64,1536]{1,0:T(8,128)(2,1)S(1)} %all_gather.3, bf16[1536,3072]{1,0:T(8,128)(2,1)S(1)} %bitcast.15), kind=kOutput, calls=%fused_computation.17 | convolution fusion | flops 603979776 | bytes 10420224 | tf_op jit(solution)/shard_map/dot_general | solution.py:21
  49.4 0.0 slice-start
  49.4 0.0 all-reduce.4.cloned.1.call-update
  49.5 44.0 %all-reduce.4.cloned.1.call-done = (f32[64,3072]{1,0:T(8,128)}, f32[64,3072]{1,0:T(8,128)}) async-done(((f32[64,3072]{1,0:T(8,128)}, f32[64,3072]{1,0:T(8,128)}), (f32[64,3072]{1,0:T(8,128)}, f32[64,3072]{1,0:T(8,128)})) %all-reduce.4.cloned.1.call-update) | async-done | bytes 1572880 | tf_op jit(solution)/shard_map/psum | solution.py:23
  93.5 0.0 slice-start.1
  93.5 0.0 slice-start.2
  93.5 0.0 copy-start
  93.5 6.3 %fusion.5 = f32[64,1536]{1,0:T(8,128)S(1)} fusion(bf16[3072,1536]{1,0:T(8,128)(2,1)} %param.8, f32[64,3072]{1,0:T(8,128)} %get-tuple-element.4, f32[64,3072]{1,0:T(8,128)} %get-tuple-element.5), kind=kOutput, calls=%fused_computation.13 | convolution fusion | flops 607715328 | bytes 11403264 | tf_op jit(solution)/shard_map/dot_general | solution.py:25
  99.8 0.0 slice-done
  99.8 0.0 slice-done.1
  99.8 0.3 slice-done.2
  100.1 0.1 copy-done
  100.2 1.8 convolution_add_fusion
  102.0 44.5 %all-reduce.5 = bf16[64,1536]{1,0:T(8,128)(2,1)S(1)} all-reduce(f32[64,1536]{1,0:T(8,128)S(1)} %convolution_add_fusion), channel_id=1, replica_groups=mesh['row'=4,'col'=2,'depth'=4] {'col','depth'}, use_global_device_ids=true, to_apply=%region_2.0 | all-reduce | flops 98304 | bytes 589824 | tf_op jit(solution)/shard_map/psum | solution.py:28
  146.5 6.6 %fusion.13 = f32[64,3072]{1,0:T(8,128)S(1)} fusion(bf16[64,1536]{1,0:T(8,128)(2,1)S(1)} %all-reduce.5, bf16[3072,1536]{1,0:T(8,128)(2,1)} %param.8), kind=kOutput, calls=%fused_computation.19 | convolution fusion | flops 603979776 | bytes 10420224 | tf_op jit(solution)/shard_map/dot_general | solution.py:29
  153.1 0.1 collective-permute-start
  153.2 2.3 %collective-permute-done = f32[64,3072]{1,0:T(8,128)S(1)} collective-permute-done((f32[64,3072]{1,0:T(8,128)S(1)}, f32[64,3072]{1,0:T(8,128)S(1)}, u32[]{:S(2)}, u32[]{:S(2)}) %collective-permute-start) | collective-permute-done | bytes 786464 | tf_op jit(solution)/shard_map/ppermute | solution.py:34
  155.5 0.1 add.33
  155.5 0.7 collective-permute-start.1
  156.3 8.3 %convolution_multiply_fusion = f32[3072,1536]{1,0:T(8,128)} fusion(bf16[64,1536]{1,0:T(8,128)(2,1)S(1)} %all-reduce.5, f32[64,3072]{1,0:T(8,128)S(1)} %copy-done), kind=kOutput, calls=%fused_computation.1 | convolution fusion | flops 610467840 | bytes 19857408 | tf_op jit(solution)/shard_map/dot_general | solution.py:38
  164.6 10.6 %collective-permute-done.1 = f32[64,3072]{1,0:T(8,128)S(1)} collective-permute-done((f32[64,3072]{1,0:T(8,128)S(1)}, f32[64,3072]{1,0:T(8,128)S(1)}, u32[]{:S(2)}, u32[]{:S(2)}) %collective-permute-start.1) | collective-permute-done | bytes 786464 | tf_op jit(solution)/shard_map/ppermute | solution.py:34
  175.2 7.9 %multiply_bitcast_fusion = f32[1536,3072]{0,1:T(8,128)} fusion(bf16[64,1536]{1,0:T(8,128)(2,1)S(1)} %all_gather.3, f32[64,3072]{1,0:T(8,128)S(1)} %add.33, f32[64,3072]{1,0:T(8,128)S(1)} %collective-permute-done.1, f32[64,3072]{1,0:T(8,128)S(1)} %copy-done), kind=kOutput, calls=%fused_computation | convolution fusion | flops 612630528 | bytes 21430272 | tf_op jit(solution)/shard_map/dot_general | solution.py:44
  183.1 18.6 %copy.7 = f32[1536,3072]{1,0:T(8,128)} copy(f32[1536,3072]{0,1:T(8,128)} %multiply_bitcast_fusion) | data formatting | bytes 37748736
  (2 shorter events, 0.0 us)
Async XLA Ops:
  7.2 39.6 %slice-start.3 = ((s8[9437184]{0:T(1024)(128)(4,1)}), s8[1048576]{0:T(1024)(128)(4,1)S(1)}, s32[]{:S(2)}) async-start(s8[9437184]{0:T(1024)(128)(4,1)} %bitcast.14), calls=%async_computation.4 | async-start | bytes 2097152
  7.2 86.3 %all-reduce.4.cloned.1.call-start = ((), (), s32[]{:S(2)}) async-start(), calls=%async_computation | async-start | bytes 3145728 | tf_op jit(solution)/shard_map/psum | solution.py:23
  40.3 6.5 %slice-start.4 = ((s8[9437184]{0:T(1024)(128)(4,1)}), s8[4194304]{0:T(1024)(128)(4,1)S(1)}, s32[]{:S(2)}) async-start(s8[9437184]{0:T(1024)(128)(4,1)} %bitcast.14), calls=%async_computation.5 | async-start | bytes 8388608
  40.3 6.5 %slice-start.5 = ((s8[9437184]{0:T(1024)(128)(4,1)}), s8[4194304]{0:T(1024)(128)(4,1)S(1)}, s32[]{:S(2)}) async-start(s8[9437184]{0:T(1024)(128)(4,1)} %bitcast.14), calls=%async_computation.6 | async-start | bytes 8388608
  49.4 50.3 %slice-start = ((s8[9437184]{0:T(1024)(128)(4,1)}), s8[1048576]{0:T(1024)(128)(4,1)S(1)}, s32[]{:S(2)}) async-start(s8[9437184]{0:T(1024)(128)(4,1)} %bitcast.12), calls=%async_computation.1 | async-start | bytes 2097152
  93.5 6.3 %slice-start.1 = ((s8[9437184]{0:T(1024)(128)(4,1)}), s8[4194304]{0:T(1024)(128)(4,1)S(1)}, s32[]{:S(2)}) async-start(s8[9437184]{0:T(1024)(128)(4,1)} %bitcast.12), calls=%async_computation.2 | async-start | bytes 8388608
  93.5 6.6 %slice-start.2 = ((s8[9437184]{0:T(1024)(128)(4,1)}), s8[4194304]{0:T(1024)(128)(4,1)S(1)}, s32[]{:S(2)}) async-start(s8[9437184]{0:T(1024)(128)(4,1)} %bitcast.12), calls=%async_computation.3 | async-start | bytes 8388608
  93.5 6.7 %copy-start = (f32[64,3072]{1,0:T(8,128)S(1)}, f32[64,3072]{1,0:T(8,128)}, u32[]{:S(2)}) copy-start(f32[64,3072]{1,0:T(8,128)} %get-tuple-element.5) | copy-start | bytes 2359300
  153.1 2.4 %collective-permute-start = (f32[64,3072]{1,0:T(8,128)S(1)}, f32[64,3072]{1,0:T(8,128)S(1)}, u32[]{:S(2)}, u32[]{:S(2)}) collective-permute-start(f32[64,3072]{1,0:T(8,128)S(1)} %fusion.13), channel_id=1, source_target_pairs={{0,8},{8,0},{16,24},{24,16},{1,9},{9,1},{17,25},{25,17},{2,10},{10... | collective-permute-start | bytes 2359304 | tf_op jit(solution)/shard_map/ppermute | solution.py:34
  155.5 19.6 %collective-permute-start.1 = (f32[64,3072]{1,0:T(8,128)S(1)}, f32[64,3072]{1,0:T(8,128)S(1)}, u32[]{:S(2)}, u32[]{:S(2)}) collective-permute-start(f32[64,3072]{1,0:T(8,128)S(1)} %add.33), channel_id=1, source_target_pairs={{0,16},{8,24},{16,0},{24,8},{1,17},{9,25},{17,1},{25,9},{2,18},{10... | collective-permute-start | bytes 2359304 | tf_op jit(solution)/shard_map/ppermute | solution.py:34
Sparse Core Ops, SparseCore 0:
  49.6 43.8 all-reduce.3
